TPU v7x, 32 devices: a whole 2x2x4 slice. The times are simulated.
32 devices in a mesh: rep: 2 (over y), fsdp: 4 (over z), seq: 4 (over x, core).
Axes of the slice: x: 2, y: 2, z: 4, core: 2. Of those that a mesh axis runs over, the one named last changes fastest.
Arguments:
- latents: bfloat16 [8, 1024, 1152], P(('rep', 'fsdp'), 'seq'), may hold values from -6 to 6
- cond: bfloat16 [8, 1152], P(('rep', 'fsdp')), may hold values from -6 to 6
- w_ada: bfloat16 [1152, 6912], P(('fsdp', 'seq')), may hold values from -0.25 to 0.25
- b_ada: bfloat16 [6912], P(('fsdp', 'seq')), may hold values from -3 to 3
- w_qkv: bfloat16 [1152, 3456], P(('fsdp', 'seq')), may hold values from -0.1875 to 0.1875
- b_qv: bfloat16 [2304], P(('fsdp', 'seq')), may hold values from -3 to 3
- w_out: bfloat16 [1152, 1152], P(('fsdp', 'seq')), may hold values from -1.5 to 1.5
- b_out: bfloat16 [1152], P(('fsdp', 'seq')), may hold values from -3 to 3
- w_one: bfloat16 [1152, 4608], P(('fsdp', 'seq')), may hold values from -0.1875 to 0.1875
- b_one: bfloat16 [4608], P(('fsdp', 'seq')), may hold values from -3 to 3
- w_two: bfloat16 [4608, 1152], P(('fsdp', 'seq')), may hold values from -0.09375 to 0.09375
- b_two: bfloat16 [1152], P(('fsdp', 'seq')), may hold values from -3 to 3
- cotangent: bfloat16 [8, 1024, 1152], P(('rep', 'fsdp'), 'seq'), may hold values from -6 to 6
Outputs:
- block_out: bfloat16 [8, 1024, 1152], P(('rep', 'fsdp'), 'seq')
- grad_latents: float32 [8, 1024, 1152], P(('rep', 'fsdp'), 'seq')
- grad_cond: float32 [8, 1152], P(('rep', 'fsdp'))
- grad_w_ada: float32 [1152, 6912], P(('fsdp', 'seq'))
- grad_b_ada: float32 [6912], P(('fsdp', 'seq'))
- grad_w_qkv: float32 [1152, 3456], P(('fsdp', 'seq'))
- grad_b_qv: float32 [2304], P(('fsdp', 'seq'))
- grad_w_out: float32 [1152, 1152], P(('fsdp', 'seq'))
- grad_b_out: float32 [1152], P(('fsdp', 'seq'))
- grad_w_one: float32 [1152, 4608], P(('fsdp', 'seq'))
- grad_b_one: float32 [4608], P(('fsdp', 'seq'))
- grad_w_two: float32 [4608, 1152], P(('fsdp', 'seq'))
- grad_b_two: float32 [1152], P(('fsdp', 'seq'))
All inputs are finite; a program needn't handle non-finite values.
Results may differ from a plain program's by a relative error of at most 0.014.
The roundings to bfloat16 on the way count: a program that leaves them out, or rounds other values in their place, can miss the bound.
Values may be sent and summed in bfloat16 or wider, within the bound.
A program may use at most 448 MiB of HBM per device.

v0:
```python
import math

import jax
import jax.numpy as jnp
from jax import lax
from jax.experimental import pallas as pl
from jax.experimental.pallas import tpu as pltpu
from jax.sharding import PartitionSpec as P

H = 16
epsilon = 1e-06
gelu_coef = math.sqrt(2.0 / math.pi)
log2e = math.log2(math.e)
BF = jnp.bfloat16
F32 = jnp.float32
LANES = 128
VM = pl.BlockSpec(memory_space=pltpu.VMEM)
HB = pl.BlockSpec(memory_space=pl.ANY)
DMA = pltpu.SemaphoreType.DMA


def params(ident, mib):
    return pltpu.CompilerParams(
        collective_id=ident, has_side_effects=True, vmem_limit_bytes=mib * 1024 * 1024
    )


def remote(src, dst, send, recv, device):
    return pltpu.make_async_remote_copy(
        src_ref=src,
        dst_ref=dst,
        send_sem=send,
        recv_sem=recv,
        device_id=device,
        device_id_type=pl.DeviceIdType.MESH,
    )


def local(src, dst, sem):
    return pltpu.make_async_copy(src, dst, sem)


def await_bytes(like, sem):
    pltpu.make_async_copy(like, like, sem).wait()


class Moves:
    def __init__(self, sem, *pairs):
        self.copies = [local(pair[0], pair[1], sem.at[i]) for i, pair in enumerate(pairs)]

    def start(self, *which):
        for i in which or range(len(self.copies)):
            self.copies[i].start()

    def wait(self, *which):
        for i in which or range(len(self.copies)):
            self.copies[i].wait()


def each(start, stop, body):
    def step(index, carry):
        body(index)
        return carry

    lax.fori_loop(start, stop, step, 0)


def greet(count, device_of):
    gate = pltpu.get_barrier_semaphore()
    each(
        1,
        count,
        lambda i: pl.semaphore_signal(
            gate, 1, device_id=device_of(i), device_id_type=pl.DeviceIdType.MESH
        ),
    )
    return count - 1


def greet_wait(count):
    pl.semaphore_wait(pltpu.get_barrier_semaphore(), count)


def norm_stats(values):
    center = values - jnp.mean(values, axis=-1, keepdims=True)
    inv_std = lax.rsqrt(jnp.mean(center * center, axis=-1, keepdims=True) + epsilon)
    return (center * inv_std, inv_std)


def norm_back(grad, normed, inv_std):
    return inv_std * (
        grad
        - jnp.mean(grad, axis=-1, keepdims=True)
        - normed * jnp.mean(grad * normed, axis=-1, keepdims=True)
    )


def mm(left, right):
    return jnp.dot(left, right, preferred_element_type=F32)


def mm_nt(left, right):
    return lax.dot_general(left, right, (((1,), (1,)), ((), ())), preferred_element_type=F32)


def mm_tn(left, right):
    return lax.dot_general(left, right, (((0,), (0,)), ((), ())), preferred_element_type=F32)


class Place:
    def __init__(self, sizes):
        self.R, self.F, self.S = sizes
        self.G = self.F * self.S
        self.y = lax.axis_index("rep")
        self.z = lax.axis_index("fsdp")
        self.s = lax.axis_index("seq")
        self.me = self.z * self.S + self.s
        self.mine = lax.rem(self.s, 2) == self.y
        self.steps = (2, 1, 3) if self.F == 4 else tuple(range(1, self.F))

    def zs(self, i):
        return lax.rem(self.z + i, self.F)

    def zs_back(self, i):
        return lax.rem(self.z - i + self.F, self.F)

    def ss(self, i):
        return lax.rem(self.s + i, self.S)

    def ss_back(self, i):
        return lax.rem(self.s - i + self.S, self.S)

    def flip(self):
        return {"rep": 1 - self.y}

    def peer(self, j):
        return lax.bitwise_xor(self.s, j)


class SeqGather:
    def __init__(self, at, dst, sem):
        self.at, self.dst, self.sem = at, dst, sem

    @staticmethod
    def scratch(S):
        return DMA((4, S))

    def direct(self, j):
        at, block = self.at, self.dst.at[self.at.s]
        return remote(block, block, self.sem.at[0, j], self.sem.at[1, j], {"seq": at.peer(j)})

    def handed(self, j):
        at = self.at
        block = self.dst.at[at.peer(j)]
        return remote(block, block, self.sem.at[2, j], self.sem.at[3, j], {"seq": at.peer(1)})

    def start(self):
        for j in range(3, self.at.S, 2):
            self.direct(j).start()
        self.direct(1).start()

    def arrive(self, index):
        @pl.when(index == 1)
        def _():
            self.direct(1).wait()

        if self.at.S > 2:

            @pl.when((index >= 2) & (lax.rem(index, 2) == 0))
            def _():
                self.direct(index + 1).wait()
                self.handed(index + 1).start()

            @pl.when((index >= 2) & (lax.rem(index, 2) == 1))
            def _():
                self.handed(index).wait()


def arrival(index):
    return jnp.where(index < 2, index, lax.bitwise_xor(index, 1))


class SeqSum:
    def __init__(self, at, src, near, inn, sem):
        self.at, self.src, self.near, self.inn, self.sem = at, src, near, inn, sem

    @staticmethod
    def scratch(S, rows, cols):
        return [
            pltpu.VMEM((S, rows, cols), BF),
            pltpu.VMEM((S // 2, rows, cols), BF),
            pltpu.VMEM((S // 2, rows, cols), BF),
            DMA((4, S)),
        ]

    def sibling(self, j):
        at = self.at
        return remote(
            self.src.at[at.peer(j)],
            self.near.at[j // 2],
            self.sem.at[0, j],
            self.sem.at[1, j],
            {"seq": at.peer(1)},
        )

    def direct(self, j):
        at = self.at
        return remote(
            self.src.at[at.peer(j)],
            self.inn.at[j // 2],
            self.sem.at[2, j],
            self.sem.at[3, j],
            {"seq": at.peer(j)},
        )

    def send(self, index):
        @pl.when((index == 1) | ((index >= 2) & (lax.rem(index, 2) == 0)))
        def _():
            self.sibling(lax.bitwise_or(index, 1)).start()

        if self.at.S > 2:

            @pl.when((index >= 2) & (lax.rem(index, 2) == 1))
            def _():
                j = index - 1
                self.sibling(index).wait()
                t = self.at.peer(j)
                step = min(64, self.src.shape[1])

                def add(i):
                    rows = pl.ds(pl.multiple_of(i * step, step), step)
                    both = self.src[t, rows, :].astype(F32) + self.near[j // 2, rows, :].astype(F32)
                    self.src[t, rows, :] = both.astype(BF)

                each(0, self.src.shape[1] // step, add)
                self.direct(j).start()

    def wait(self):
        self.sibling(1).wait()
        for j in range(2, self.at.S, 2):
            self.direct(j).wait()

    def total(self, rows):
        value = self.src[self.at.s, rows, :].astype(F32) + self.near[0, rows, :].astype(F32)
        for k in range(1, self.at.S // 2):
            value = value + self.inn[k, rows, :].astype(F32)
        return value


class FarGather:
    relayed = True

    def __init__(self, at, dst, sem):
        self.at, self.dst, self.sem = at, dst, sem
        self.line = self.relayed and at.F == 4

    @staticmethod
    def scratch(F):
        return DMA((7, F))

    def send(self, z_from, z_to, kind):
        pieces = self.half(z_from)
        held = self.origin() if kind == 0 else pieces
        for source, piece in zip(held, pieces):
            remote(
                source, piece, self.sem.at[kind, z_to], self.sem.at[2, z_from], {"fsdp": z_to}
            ).start()

    def origin(self):
        return self.half(self.at.z)

    def await_half(self, row, z):
        await_bytes(self.like(), self.sem.at[row, z])

    def around(self, step, body):
        at = self.at

        @pl.when(at.z >= step)
        def _():
            body(at.z - step)

        @pl.when(at.z + step < at.F)
        def _():
            body(at.z + step)

    def direct(self, step, body):
        if self.line and step == 3:
            return
        self.around(step, body)

    def start_far(self):
        for step in self.at.steps:
            self.direct(step, lambda z_to: self.send(self.at.z, z_to, 0))

    def service(self, step):
        at = self.at

        def take(z_from):
            self.await_half(2, z_from)
            for piece in self.half(z_from):
                remote(
                    piece, piece, self.sem.at[3, z_from], self.sem.at[4, z_from], at.flip()
                ).start()

        self.around(step, take)
        if self.line and step == 2:

            @pl.when((at.z == 1) | (at.z == 2))
            def _():
                far = jnp.where(at.z == 1, 3, 0)
                end = 3 - far
                self.send(far, end, 1)

    def finish_far(self):
        at = self.at

        def swapped(z_from):
            self.await_half(3, z_from)
            self.await_half(4, z_from)

        for step in range(1, at.F):
            self.around(step, swapped)
            self.direct(step, lambda z_to: self.await_half(0, z_to))
        if self.line:

            @pl.when((at.z == 1) | (at.z == 2))
            def _():
                self.await_half(1, jnp.where(at.z == 1, 0, 3))


class ColumnGather(FarGather):
    def __init__(self, at, src, dst, sem):
        super().__init__(at, dst, sem)
        self.src = src

    def half(self, z):
        at = self.at
        return [self.dst.at[z * at.S + 2 * k + at.y] for k in range(at.S // 2)]

    def like(self):
        return self.dst.at[pl.ds(0, self.at.S // 2)]

    def start(self):
        at, src, dst, sem = self.at, self.src, self.dst, self.sem

        def near(j):
            t = at.ss(j)
            remote(src.at[t], dst.at[at.me], sem.at[5, 0], sem.at[6, 0], {"seq": t}).start()

        each(1, at.S, near)
        local(src.at[at.s], dst.at[at.me], sem.at[5, 1]).start()

    def near_done(self):
        at, dst, sem = self.at, self.dst, self.sem
        local(self.src.at[at.s], dst.at[at.me], sem.at[5, 1]).wait()
        near = dst.at[pl.ds(0, at.S - 1)]
        await_bytes(near, sem.at[5, 0])
        await_bytes(near, sem.at[6, 0])


class RowGather(FarGather):
    def __init__(self, at, src, dst, sem):
        super().__init__(at, dst, sem)
        self.src = src

    def half(self, z):
        return [self.dst.at[z, self.at.y]]

    def origin(self):
        return [self.src.at[self.at.y]]

    def like(self):
        return self.dst.at[0, 0]

    def start(self):
        at = self.at
        local(self.src, self.dst.at[at.z], self.sem.at[5, 0]).start()

    def near_done(self):
        at = self.at
        local(self.src, self.dst.at[at.z], self.sem.at[5, 0]).wait()


class OwnGather(FarGather):
    relayed = False

    def __init__(self, at, src, dst, sem):
        super().__init__(at, dst, sem)
        self.src = src

    def half(self, z):
        return [self.dst.at[self.at.s, z]]

    def origin(self):
        return [self.src]

    def like(self):
        return self.src

    def start(self):
        at = self.at
        local(self.src, self.dst.at[at.s, at.z], self.sem.at[5, 0]).start()

    def near_done(self):
        at = self.at
        local(self.src, self.dst.at[at.s, at.z], self.sem.at[5, 0]).wait()

    def start_far(self):
        pl.when(self.at.mine)(super().start_far)

    def service(self, step):
        take = super().service
        pl.when(self.at.mine)(lambda: take(step))

    def finish_far(self):
        at = self.at

        def sent(z_from):
            self.await_half(3, z_from)

        def swapped(z_from):
            self.await_half(4, z_from)

        @pl.when(at.mine)
        def _():
            for step in range(1, at.F):
                self.around(step, sent)
                self.direct(step, lambda z_to: self.await_half(0, z_to))
            if self.line:

                @pl.when((at.z == 1) | (at.z == 2))
                def _():
                    self.await_half(1, jnp.where(at.z == 1, 0, 3))

        @pl.when(jnp.logical_not(at.mine))
        def _():
            for step in range(1, at.F):
                self.around(step, swapped)


def forward_kernel(sizes, *refs):
    at = Place(sizes)
    R, F, S, G = at.R, at.F, at.S, at.G
    cond, biases = refs[:2]
    i_latents, i_cotangent, i_ada, i_qkv, i_one, w_two, w_out = refs[2:9]
    refs = refs[:1] + refs
    o_mixed, o_heads, o_merged, o_branch, o_mix, o_grad, o_full_qkv, o_full_out = refs[10:18]
    log_sums, mod, silu_all, bias_one, bias_two, g_one, g_two = refs[18:25]
    silu_src, part, parts_in, mod_src, mod_in, qkv_src, one_src, pack_all = refs[25:33]
    g_qkv, g_out, wide, bias_qkv, bias_out, val_flip, att, merged_in = refs[33:41]
    silu_sem, part_sem, mod_sem, pack_sem, qkv_sem, one_sem, two_sem, out_sem = refs[41:49]
    mixed_sem, grad_sem, att_sem, mix_sem, spread_sem, load_sem, save_sem = refs[49:56]
    bias_pack, bias_pieces, bias_slot = refs[69:72]
    latents, cotangent, w_ada, w_qkv, w_one = refs[56:61]
    mixed_all, heads, merged, branch_one, mix_all, grad_all, full_qkv, full_out = refs[61:69]
    loads = Moves(
        load_sem,
        (i_qkv, w_qkv),
        (i_ada, w_ada),
        (i_one, w_one),
        (i_latents, latents),
        (i_cotangent, cotangent),
    )
    loads.start()
    saves = Moves(
        save_sem,
        (mixed_all, o_mixed),
        (heads, o_heads),
        (merged, o_merged),
        (branch_one, o_branch),
        (mix_all, o_mix),
        (grad_all, o_grad),
        (full_qkv, o_full_qkv),
        (full_out, o_full_out),
    )
    L, D = latents.shape
    C = D // S
    T = S * L
    local_heads = H // S
    size = D // H
    rows_own = silu_all.shape[2]
    hidden = one_src.shape[2]
    block = hidden // F
    greet(G, lambda i: {"fsdp": lax.rem(at.me + i, G) // S, "seq": lax.rem(at.me + i, S)})
    greet(2 * F, lambda i: {"rep": lax.rem(at.y + i // F, 2), "fsdp": at.zs(i)})
    width = bias_pieces.shape[2]
    bias_pack[...] = biases[:, width:].astype(F32)
    bias_pieces[...] = jnp.zeros_like(bias_pieces)
    bias_pieces[at.me] = biases[:, :width].astype(F32)
    for g in range(G):
        bias_slot[:, g * width : (g + 1) * width] = bias_pieces[g]

    value = cond[...].astype(F32)
    silu = (value * jax.nn.sigmoid(value)).astype(BF).astype(F32)
    for g in range(G):
        silu_src[g] = silu[:, g * rows_own : (g + 1) * rows_own]
    loads.wait(0)
    for t in range(S):
        for j in range(3):
            qkv_src[t, :, j * C : (j + 1) * C] = w_qkv[:, j * D + t * C : j * D + (t + 1) * C]
    loads.wait(2)
    for t in range(S):
        for f in range(F):
            col = (f * S + t) * block
            one_src[t, :, f * block : (f + 1) * block] = w_one[:, col : col + block]
    greet_wait(G - 1 + 2 * F - 1)
    slot = at.y * F + at.z

    def cond_copy(i):
        z_to = at.zs(i)
        return remote(
            silu_src.at[z_to * S + at.s],
            silu_all.at[slot],
            silu_sem.at[0, i],
            silu_sem.at[1, i],
            {"rep": lax.rem(at.y + i // F, 2), "fsdp": z_to},
        )

    each(1, 2 * F, lambda i: cond_copy(i).start())
    silu_all[slot] = silu_src[at.me]

    def pack_copy(i):
        to = lax.rem(at.me + i, G)
        return remote(
            bias_pack,
            pack_all.at[at.me],
            pack_sem.at[0, 0],
            pack_sem.at[1, 0],
            {"fsdp": to // S, "seq": lax.rem(to, S)},
        )

    each(1, G, lambda i: pack_copy(i).start())
    pack_all[at.me] = bias_pack[...]

    qkv = ColumnGather(at, qkv_src, g_qkv, qkv_sem)
    one = ColumnGather(at, one_src, g_one, one_sem)
    two = RowGather(at, w_two, g_two, two_sem)
    out = OwnGather(at, w_out, g_out, out_sem)
    qkv.start()
    two.start()
    out.start()

    each(1, 2 * F, lambda i: cond_copy(i).wait())
    left = jnp.concatenate([silu_all[at.y * F + f] for f in range(F)], axis=0).astype(BF)
    loads.wait(1)
    sums = mm(left, w_ada[...]) + bias_slot[...]
    for f in range(F):
        for v in range(6):
            for t in range(S):
                col = v * D + t * C
                part[f * S + t, v : v + 1, :] = sums[f : f + 1, col : col + C]

    def part_copy(i):
        to = lax.rem(at.me + i, G)
        return remote(
            part.at[to],
            parts_in.at[at.me],
            part_sem.at[0, i],
            part_sem.at[1, i],
            {"fsdp": to // S, "seq": lax.rem(to, S)},
        )

    each(1, G, lambda i: part_copy(i).start())
    parts_in[at.me] = part[at.me]
    qkv.near_done()
    qkv.start_far()
    each(1, G, lambda i: part_copy(i).wait())
    total = parts_in[0]
    for g in range(1, G):
        total = total + parts_in[g]
    mod_src[...] = total

    def mod_copy(i):
        return remote(
            mod_src, mod_in.at[at.s], mod_sem.at[0, i], mod_sem.at[1, i], {"seq": at.ss(i)}
        )

    each(1, S, lambda i: mod_copy(i).start())
    one.start()
    mod_in[at.s] = total
    out.start_far()
    each(1, S, lambda i: mod_copy(i).wait())
    for t in range(S):
        mod[:, t * C : (t + 1) * C] = mod_in[t]

    loads.wait(3)
    step = min(64, L)

    def norm(i):
        at_rows = pl.ds(pl.multiple_of(i * step, step), step)
        normed, _ = norm_stats(latents[at_rows, :].astype(F32))
        mixed_all[at.s, at_rows, :] = (normed * (1.0 + mod[1:2, :]) + mod[0:1, :]).astype(BF)

    each(0, L // step, norm)
    gather = SeqGather(at, mixed_all, mixed_sem)
    gather.start()
    loads.wait(4)
    grad_all[at.s] = (mod[5:6, :] * cotangent[...].astype(F32)).astype(BF)
    grad_gather = SeqGather(at, grad_all, grad_sem)
    grad_gather.start()
    one.near_done()
    qkv.service(at.steps[0])
    one.start_far()
    out.near_done()
    two.near_done()

    others = pack_all.at[pl.ds(0, G - 1)]
    await_bytes(others, pack_sem.at[0, 0])
    await_bytes(others, pack_sem.at[1, 0])
    qv = 2 * D // G
    own = F // 2
    bias_qkv[...] = jnp.zeros_like(bias_qkv)
    for i in range(own):
        bias_qkv[:, i * qv : (i + 1) * qv] = pack_all[at.s * own + i][:, 0:qv]
        bias_qkv[:, 2 * C + i * qv : 2 * C + (i + 1) * qv] = pack_all[G // 2 + at.s * own + i][
            :, 0:qv
        ]
    for g in range(G):
        cols = slice(g * rows_own, (g + 1) * rows_own)
        bias_out[:, cols] = pack_all[g][:, qv : qv + rows_own]
        bias_two[:, cols] = pack_all[g][:, qv + rows_own : qv + 2 * rows_own]
    for f in range(F):
        bias_one[:, f * block : (f + 1) * block] = pack_all[f * S + at.s][:, qv + 2 * rows_own :]

    for i in at.steps[1:]:
        qkv.service(i)
    for i in at.steps:
        out.service(i)
    qkv.finish_far()

    def join(slabs, whole):
        cols = whole.shape[1]
        for g in range(G):
            wide[g * rows_own : (g + 1) * rows_own, 0:cols] = slabs(g).astype(F32)
        tall = 128 if D % 128 == 0 else D

        def cast(i):
            at_rows = pl.ds(pl.multiple_of(i * tall, tall), tall)
            whole[at_rows, :] = wide[at_rows, 0:cols].astype(BF)

        each(0, D // tall, cast)

    join(lambda g: g_qkv[g], full_qkv)
    saves.start(6)

    pad = jnp.zeros((L, LANES - size), BF)

    def project(index):
        gather.arrive(index)
        t = at.peer(arrival(index))
        at_rows = pl.ds(pl.multiple_of(t * L, L), L)
        done = (mm(mixed_all[t], full_qkv[...]) + bias_qkv[...]).astype(BF)
        for c in range(3 * local_heads):
            heads[c, at_rows, :] = jnp.concatenate(
                [done[:, c * size : (c + 1) * size], pad], axis=1
            )

    each(0, S, project)
    saves.start(0, 1)
    out.finish_far()
    spread = SeqGather(at, g_out, spread_sem)
    spread.start()
    each(1, S, grad_gather.arrive)
    saves.start(5)
    for h in range(local_heads):
        val_flip[h] = heads[2 * local_heads + h].T

    def att_copy(j):
        t = at.peer(j)
        return remote(
            att.at[t], merged_in.at[at.s], att_sem.at[0, j], att_sem.at[1, j], {"seq": t}
        )

    factor = size ** (-0.5) * log2e

    def attention(index):
        j = S - 1 - index
        t = at.peer(j)
        at_rows = pl.ds(pl.multiple_of(t * L, L), L)
        for h in range(local_heads):
            scores = mm_nt(heads[local_heads + h], heads[h, at_rows, :]) * factor
            highest = jnp.max(scores, axis=0, keepdims=True)
            raised = jnp.exp2(scores - highest)
            summed = jnp.sum(raised, axis=0, keepdims=True)
            result = mm(val_flip[h], raised.astype(BF)) / summed
            log_sums[h, t] = highest + jnp.log2(summed)
            att[t, :, h * size : (h + 1) * size] = result.T[:, :size].astype(BF)

        @pl.when(j > 0)
        def _():
            att_copy(j).start()

    one.service(at.steps[0])
    one.service(at.steps[1])
    two.start_far()
    each(0, S, attention)
    merged_in[at.s] = att[at.s]
    each(1, S, spread.arrive)
    join(lambda g: g_out[g % S, g // S], full_out)
    saves.start(7)
    each(1, S, lambda j: att_copy(j).wait())
    for t in range(S):
        merged[:, t * C : (t + 1) * C] = merged_in[t]
    saves.start(2)

    def project_out(i):
        at_rows = pl.ds(pl.multiple_of(i * step, step), step)
        branch = mm(merged[at_rows, :], full_out[...]) + bias_out[...]
        branch_one[at_rows, :] = branch
        residual = latents[at_rows, :].astype(F32) + mod[2:3, :] * branch
        normed, _ = norm_stats(residual)
        mix_all[at.s, at_rows, :] = (normed * (1.0 + mod[4:5, :]) + mod[3:4, :]).astype(BF)

    each(0, L // step, project_out)
    saves.start(3)
    mix_gather = SeqGather(at, mix_all, mix_sem)
    mix_gather.start()
    for i in at.steps[2:]:
        one.service(i)
    for i in at.steps:
        two.service(i)
    one.finish_far()
    each(1, S, mix_gather.arrive)
    saves.start(4)
    two.finish_far()
    saves.wait()


def forward(sizes, cond, biases, latents, cotangent, w_ada, w_qkv, w_one, w_two, w_out):
    R, F, S = sizes
    G = F * S
    rows, D = w_out.shape
    L = latents.shape[0]
    T = S * L
    C = D // S
    local_heads = H // S
    hidden = w_one.shape[1] // S
    shape = jax.ShapeDtypeStruct
    width = 6 * D // G
    pack = biases.shape[1] - width
    kept = (
        ((S, L, D), BF),
        ((3 * local_heads, T, LANES), BF),
        ((L, D), BF),
        ((L, D), F32),
        ((S, L, D), BF),
        ((S, L, D), BF),
        ((D, 3 * C), BF),
        ((D, D), BF),
    )
    return pl.pallas_call(
        lambda *refs: forward_kernel(sizes, *refs),
        name="forward",
        out_shape=tuple(shape(*item) for item in kept)
        + (
            shape((local_heads, S, 1, L), F32),
            shape((6, D), F32),
            shape((R * F, 1, rows), F32),
            shape((1, hidden), F32),
            shape((1, D), F32),
            shape((G, rows, hidden), BF),
            shape((F,) + w_two.shape, BF),
        ),
        in_specs=[VM] * 2 + [HB] * 7,
        out_specs=(HB,) * 8 + (VM,) * 5 + (HB,) * 2,
        scratch_shapes=[
            pltpu.VMEM((G, 1, rows), F32),
            pltpu.VMEM((G, 6, C), F32),
            pltpu.VMEM((G, 6, C), F32),
            pltpu.VMEM((6, C), F32),
            pltpu.VMEM((S, 6, C), F32),
            pltpu.VMEM((S, rows, 3 * C), BF),
            pltpu.VMEM((S, rows, hidden), BF),
            pltpu.VMEM((G, 1, pack), F32),
            pltpu.VMEM((G, rows, 3 * C), BF),
            pltpu.VMEM((S, F, rows, D), BF),
            pltpu.VMEM((D, max(D, 3 * C)), F32),
            pltpu.VMEM((1, 3 * C), F32),
            pltpu.VMEM((1, D), F32),
            pltpu.VMEM((local_heads, LANES, T), BF),
            pltpu.VMEM((S, L, C), BF),
            pltpu.VMEM((S, L, C), BF),
            DMA((2, 2 * F)),
            DMA((2, G)),
            DMA((2, S)),
            DMA((2, 1)),
            ColumnGather.scratch(F),
            ColumnGather.scratch(F),
            RowGather.scratch(F),
            OwnGather.scratch(F),
            SeqGather.scratch(S),
            SeqGather.scratch(S),
            DMA((2, S)),
            SeqGather.scratch(S),
            SeqGather.scratch(S),
            DMA((5,)),
            DMA((8,)),
        ]
        + [pltpu.VMEM(x.shape, x.dtype) for x in (latents, cotangent, w_ada, w_qkv, w_one)]
        + [pltpu.VMEM(*item) for item in kept]
        + [
            pltpu.VMEM((1, pack), F32),
            pltpu.VMEM((G, 1, width), F32),
            pltpu.VMEM((1, 6 * D), F32),
        ],
        compiler_params=params(1, 60),
    )(cond, biases, latents, cotangent, w_ada, w_qkv, w_one, w_two, w_out)


class RowScatter:
    def __init__(self, at, src, got, stage, sem):
        self.at, self.src, self.got, self.stage, self.sem = at, src, got, stage, sem

    def start(self):
        at = self.at

        def far(i):
            z_to = at.zs(i)
            remote(
                self.src.at[z_to, 3 - at.y],
                self.got.at[z_to],
                self.sem.at[0, i],
                self.sem.at[1, i],
                at.flip(),
            ).start()

        each(0, at.F, far)

    def reduce(self):
        at = self.at

        def far(i):
            z_to = at.zs(i)
            await_bytes(self.got.at[0], self.sem.at[0, i])
            await_bytes(self.got.at[0], self.sem.at[1, i])
            total = self.src[z_to, 2 + at.y].astype(F32) + self.got[z_to].astype(F32)
            self.stage[z_to] = total.astype(BF)

        each(0, at.F, far)


class Line:
    def line_up(self):
        at = self.at
        self.line = at.F == 4
        self.inner = self.line & ((at.z == 1) | (at.z == 2))
        self.end = self.line & ((at.z == 0) | (at.z == 3))
        self.opposite = jnp.where(at.z < 2, 3, 0)
        self.beside = jnp.where(at.z == 0, 1, 2)


class RowOwner(Line):
    def __init__(self, at, piece, inn, far, sem):
        self.at, self.piece, self.inn, self.far, self.sem = at, piece, inn, far, sem
        self.line_up()

    @staticmethod
    def scratch(F, shape):
        return [pltpu.VMEM((F,) + shape, BF), pltpu.VMEM(shape, BF), DMA((3, F))]

    def out_copy(self, z_to):
        at = self.at
        return remote(
            self.piece(z_to),
            self.inn.at[at.z],
            self.sem.at[0, z_to],
            self.sem.at[1, at.z],
            {"fsdp": z_to},
        )

    def far_copy(self):
        return remote(
            self.piece(self.opposite),
            self.far,
            self.sem.at[0, self.opposite],
            self.sem.at[2, 0],
            {"fsdp": self.beside},
        )

    def start(self):
        at = self.at

        @pl.when(self.end)
        def _():
            self.far_copy().start()
            self.inn[self.opposite] = jnp.zeros_like(self.far)

        def one(i):
            z_to = at.zs(i)

            @pl.when(jnp.logical_not(self.line & (z_to == self.opposite)))
            def _():
                self.out_copy(z_to).start()

        each(1, at.F, one)
        self.inn[at.z] = self.piece(at.z)[...]

    def relay(self):
        @pl.when(self.inner)
        def _():
            await_bytes(self.far, self.sem.at[2, 0])
            z_to = self.opposite
            piece = self.piece(z_to)
            piece[...] = (piece[...].astype(F32) + self.far[...].astype(F32)).astype(BF)
            self.out_copy(z_to).start()

    def total(self):
        at = self.at

        def arrived(i):
            z = at.zs(i)
            await_bytes(self.far, self.sem.at[0, z])

            @pl.when(jnp.logical_not(self.end & (z == self.opposite)))
            def _():
                await_bytes(self.far, self.sem.at[1, z])

        each(1, at.F, arrived)
        total = self.inn[0].astype(F32)
        for f in range(1, at.F):
            total = total + self.inn[f].astype(F32)
        return total.astype(BF)


class Swap:
    def __init__(self, at, done, sem):
        self.at, self.done, self.sem = at, done, sem

    def copy(self):
        mine = self.done.at[self.at.y]
        return remote(mine, mine, self.sem.at[0], self.sem.at[1], self.at.flip())

    def start(self):
        self.copy().start()

    def finish(self):
        self.copy().wait()


class FullScatter:
    def __init__(self, at, src, near, got, stage, inn, done, sem):
        self.at, self.src, self.near, self.got, self.stage = at, src, near, got, stage
        self.inn, self.done, self.sem = inn, done, sem

    @staticmethod
    def scratch(sizes, rows, cols):
        R, F, S = sizes
        return [
            pltpu.VMEM((S // 2, F, rows, cols), BF),
            pltpu.VMEM((S // 2, F, rows, cols), BF),
            pltpu.VMEM((F, rows, cols), BF),
            pltpu.VMEM((F, rows, cols), BF),
            DMA((10, max(F, S))),
        ]

    def sibling(self, j):
        at = self.at
        return remote(
            self.src.at[at.peer(j)],
            self.near.at[j // 2],
            self.sem.at[0, j],
            self.sem.at[1, j],
            {"seq": at.peer(1)},
        )

    def direct(self, j):
        at = self.at
        return remote(
            self.near.at[j // 2],
            self.got.at[j // 2],
            self.sem.at[2, j],
            self.sem.at[3, j],
            {"seq": at.peer(j)},
        )

    def start(self):
        for j in range(3, self.at.S, 2):
            self.sibling(j).start()
        self.sibling(1).start()

    def cross(self):
        at = self.at
        for j in range(2, at.S, 2):
            self.sibling(j + 1).wait()
            k = j // 2

            def add(f):
                both = self.near[k, f].astype(F32) + self.src[at.peer(j), f].astype(F32)
                self.near[k, f] = both.astype(BF)

            each(0, at.F, add)
            self.direct(j).start()
        self.sibling(1).wait()

    def out_copy(self, i):
        at = self.at
        return remote(
            self.stage.at[at.zs(i)],
            self.inn.at[at.z],
            self.sem.at[4, i],
            self.sem.at[5, i],
            {"fsdp": at.zs(i)},
        )

    def scatter(self):
        at = self.at
        for j in range(2, at.S, 2):
            self.direct(j).wait()

        def far(i):
            z_to = at.zs(i)
            total = self.src[at.s, z_to].astype(F32) + self.near[0, z_to].astype(F32)
            for k in range(1, at.S // 2):
                total = total + self.got[k, z_to].astype(F32)
            self.stage[z_to] = total.astype(BF)

            @pl.when(i > 0)
            def _():
                self.out_copy(i).start()

        each(0, at.F, far)
        self.inn[at.z] = self.stage[at.z]

    def total(self):
        at = self.at
        each(1, at.F, lambda i: self.out_copy(i).wait())
        total = self.inn[0].astype(F32)
        for f in range(1, at.F):
            total = total + self.inn[f].astype(F32)
        self.done[at.y] = total.astype(BF)
        mine = self.done.at[at.y]
        remote(mine, mine, self.sem.at[6, 0], self.sem.at[7, 0], at.flip()).start()

    def finish(self):
        await_bytes(self.done.at[0], self.sem.at[6, 0])
        await_bytes(self.done.at[0], self.sem.at[7, 0])


def mlp_kernel(sizes, *refs):
    at = Place(sizes)
    R, F, S, G = at.R, at.F, at.S, at.G
    mod, bias_one, bias_two = refs[:3]
    given = refs[3:12]
    block_out, o_resid, o_heads, o_w_one, o_two_sum, o_two_part, o_out_g = refs[12:19]
    refs = refs[:11] + refs[12:]
    grad_b_one, grad_b_two, grad_b_out, mod_sums = refs[18:22]
    act_all, pre_wide, pre_all, grad_branch, wide, two_g, two_got, two_sem = refs[22:30]
    branch_refs, mix_refs = refs[30:34], refs[34:38]
    two_inn, two_far, part_sem, load_sem, save_sem = refs[38:43]
    held = refs[43:52]
    w_one, mix_all, w_two, grad_all, latents, branch_one, cotangent, w_out, merged = held
    grad_resid, grad_heads, grad_w_one, two_sum, two_part, out_g = refs[52:58]
    loads = Moves(load_sem, *zip(given, held))
    loads.start()
    saves = Moves(
        save_sem,
        (grad_w_one, o_w_one),
        (grad_resid, o_resid),
        (grad_heads, o_heads),
        (out_g, o_out_g),
        (two_sum, o_two_sum),
        (two_part, o_two_part),
    )
    _, L, D = mix_all.shape
    C = D // S
    hidden = w_one.shape[1]
    tokens = S * L
    greet(S, lambda i: {"seq": at.ss(i)})
    greet(2, lambda i: at.flip())
    greet(F, lambda i: {"fsdp": at.zs(i)})
    greet_wait(S + F - 1)
    gate_one = mod[2:3, :]
    scale = mod[4:5, :]
    gate_two = mod[5:6, :]
    branch_sum = SeqSum(at, *branch_refs)
    mix_sum = SeqSum(at, *mix_refs)
    branch_src = branch_refs[0]
    mix_src = mix_refs[0]
    two = RowScatter(at, two_g, two_got, two_sum, two_sem)
    part_two = RowOwner(at, lambda z: two_g.at[z, pl.ds(0, 2)], two_inn, two_far, part_sem)
    step = min(256, L)

    def ahead(order):
        index = lax.rem(order + 2, S)
        t = at.peer(arrival(index))

        def part(i):
            rows = pl.ds(pl.multiple_of(i * step, step), step)
            pre = mm(mix_all[t, rows, :], w_one[...]) + bias_one[...]
            pre_wide[t, rows, :] = pre
            inner = gelu_coef * (pre + 0.044715 * pre * pre * pre)
            act = (0.5 * pre * (1.0 + jnp.tanh(inner))).astype(BF)
            act_all[t, rows, :] = act
            branch_src[t, rows, :] = mm(act, w_two[...]).astype(BF)

        each(0, L // step, part)
        branch_sum.send(index)

    loads.wait(0, 1, 2)
    each(0, S, ahead)
    loads.wait(3)
    column = 384 if hidden % 384 == 0 else hidden
    for i in range(hidden // column):
        cols = slice(i * column, (i + 1) * column)
        wide[cols, :] = mm_tn(
            act_all[:, :, cols].reshape(tokens, column), grad_all[...].reshape(tokens, D)
        )
    part_rows = two_g.shape[2]
    for f in range(F):
        for quarter in range(4):
            first = (4 * f + quarter) * part_rows
            two_g[f, quarter] = wide[first : first + part_rows, :].astype(BF)
    part_two.start()
    two.start()

    def behind(order):
        index = lax.rem(order + 2, S)
        t = at.peer(arrival(index))

        def part(i):
            rows = pl.ds(pl.multiple_of(i * step, step), step)
            pre = pre_wide[t, rows, :]
            square = pre * pre
            tanh_val = jnp.tanh(gelu_coef * (pre + 0.044715 * square * pre))
            slope = 0.5 * (1.0 + tanh_val) + 0.5 * pre * (
                1.0 - tanh_val * tanh_val
            ) * gelu_coef * (1.0 + 3.0 * 0.044715 * square)
            grad_pre = (mm_nt(grad_all[t, rows, :], w_two[...]) * slope).astype(BF)
            pre_all[t, rows, :] = grad_pre
            mix_src[t, rows, :] = mm_nt(grad_pre, w_one[...]).astype(BF)

        each(0, L // step, part)
        mix_sum.send(index)

        @pl.when(order == S - 1)
        def _():
            part_two.relay()

    each(0, S, behind)
    for i in range(hidden // column):
        cols = slice(i * column, (i + 1) * column)
        grads = pre_all[:, :, cols].reshape(tokens, column)
        grad_w_one[:, cols] = mm_tn(mix_all[...].reshape(tokens, D), grads).astype(BF)
        grad_b_one[:, cols] = jnp.sum(grads.astype(F32), axis=0, keepdims=True)
    grad_b_two[...] = jnp.sum(grad_all[at.s].astype(F32), axis=0, keepdims=True)
    saves.start(0)
    loads.wait(4, 5, 6, 7, 8)

    mix_sum.wait()
    step_back = min(32, L)
    mod_sums[...] = jnp.zeros_like(mod_sums)
    grad_b_out[...] = jnp.zeros_like(grad_b_out)

    def back(i):
        rows = pl.ds(pl.multiple_of(i * step_back, step_back), step_back)
        grad_mixed = mix_sum.total(rows)
        branch = branch_one[rows, :]
        residual = latents[rows, :].astype(F32) + gate_one * branch
        normed, inv_std = norm_stats(residual)
        grad_out = cotangent[rows, :].astype(F32)
        grad = grad_out + norm_back(grad_mixed * (1.0 + scale), normed, inv_std)
        grad_resid[rows, :] = grad
        low = (gate_one * grad).astype(BF)
        grad_branch[rows, :] = low
        mod_sums[2:3, :] += jnp.sum(grad * branch, axis=0, keepdims=True)
        mod_sums[3:4, :] += jnp.sum(grad_mixed, axis=0, keepdims=True)
        mod_sums[4:5, :] += jnp.sum(grad_mixed * normed, axis=0, keepdims=True)
        grad_b_out[...] += jnp.sum(low.astype(F32), axis=0, keepdims=True)

    each(0, L // step_back, back)
    grad_merged = mm_nt(grad_branch[...], w_out[...]).astype(BF)
    for t in range(S):
        grad_heads[t] = grad_merged[:, t * C : (t + 1) * C]
    saves.start(1, 2)
    for i in range(D // 384):
        cols = slice(i * 384, (i + 1) * 384)
        wide[:D, cols] = mm_tn(merged[...], grad_branch[:, cols])
    rows_own = out_g.shape[2]
    for f in range(F):
        for t in range(S):
            first = (f * S + t) * rows_own
            out_g[t, f] = wide[first : first + rows_own, :].astype(BF)
    saves.start(3)

    branch_sum.wait()

    def finish(i):
        rows = pl.ds(pl.multiple_of(i * step_back, step_back), step_back)
        branch_two = branch_sum.total(rows) + bias_two[...]
        residual = latents[rows, :].astype(F32) + gate_one * branch_one[rows, :]
        block_out[rows, :] = (residual + gate_two * branch_two).astype(BF)
        grad_out = cotangent[rows, :].astype(F32)
        mod_sums[5:6, :] += jnp.sum(grad_out * branch_two, axis=0, keepdims=True)

    each(0, L // step_back, finish)
    two.reduce()
    saves.start(4)
    two_part[...] = part_two.total()
    saves.start(5)
    saves.wait()


def mlp(sizes, *args):
    R, F, S = sizes
    G = F * S
    D, hidden = args[3].shape
    L = args[7].shape[0]
    C = D // S
    quarter = hidden // F // 4
    shape = jax.ShapeDtypeStruct
    kept = (
        ((L, D), F32),
        ((S, L, C), BF),
        ((D, hidden), BF),
        ((F, quarter, D), BF),
        ((2, quarter, D), BF),
        ((S, F, D // G, D), BF),
    )
    return pl.pallas_call(
        lambda *refs: mlp_kernel(sizes, *refs),
        name="mlp",
        out_shape=(shape((L, D), BF),)
        + tuple(shape(*item) for item in kept)
        + (
            shape((1, hidden), F32),
            shape((1, D), F32),
            shape((1, D), F32),
            shape((6, D), F32),
        ),
        in_specs=[VM] * 3 + [HB] * 9,
        out_specs=(VM,) + (HB,) * 6 + (VM,) * 4,
        scratch_shapes=[
            pltpu.VMEM((S, L, hidden), BF),
            pltpu.VMEM((S, L, hidden), F32),
            pltpu.VMEM((S, L, hidden), BF),
            pltpu.VMEM((L, D), BF),
            pltpu.VMEM((max(hidden, D), D), F32),
            pltpu.VMEM((F, 4, quarter, D), BF),
            pltpu.VMEM((F, quarter, D), BF),
            DMA((2, F)),
        ]
        + SeqSum.scratch(S, L, D)
        + SeqSum.scratch(S, L, D)
        + RowOwner.scratch(F, (2, quarter, D))
        + [DMA((9,)), DMA((6,))]
        + [pltpu.VMEM(x.shape, x.dtype) for x in args[3:]]
        + [pltpu.VMEM(*item) for item in kept],
        compiler_params=params(3, 60),
    )(*args)


class ColumnScatter:
    def __init__(self, at, src, got, stage, inn, far, along_sem, summed, done, sem):
        self.at, self.src, self.got, self.stage = at, src, got, stage
        self.summed, self.done, self.sem = summed, done, sem
        self.along = RowOwner(at, lambda z: stage.at[z], inn, far, along_sem)

    @staticmethod
    def scratch(sizes, rows, cols):
        R, F, S = sizes
        shape = (S // 2, rows, cols)
        return (
            [pltpu.VMEM((F,) + shape, BF), pltpu.VMEM((F,) + shape, BF)]
            + RowOwner.scratch(F, shape)
            + [pltpu.VMEM(shape, BF), DMA((5, F))]
        )

    def start(self):
        at = self.at

        def far(i):
            z_to = at.zs(i)

            def one(k):
                slot = z_to * at.S + 2 * k + at.y
                local(self.src.at[slot], self.stage.at[z_to, k], self.sem.at[2, i]).start()
                remote(
                    self.src.at[z_to * at.S + 2 * k + 1 - at.y],
                    self.got.at[z_to, k],
                    self.sem.at[0, i],
                    self.sem.at[1, i],
                    at.flip(),
                ).start()

            each(0, at.S // 2, one)

        each(0, at.F, far)

    def scatter(self):
        at = self.at

        def step(i):
            z_to = at.zs(i)
            await_bytes(self.got.at[0], self.sem.at[1, i])
            await_bytes(self.got.at[0], self.sem.at[2, i])

            def one(k):
                total = self.stage[z_to, k].astype(F32) + self.got[z_to, k].astype(F32)
                self.stage[z_to, k] = total.astype(BF)

            each(0, at.S // 2, one)

        each(0, at.F, step)
        self.along.start()

    def relay(self):
        self.along.relay()

    def near(self):
        at = self.at
        self.summed[...] = self.along.total()

        def one(k):
            s_to = 2 * k + at.y

            @pl.when(s_to == at.s)
            def _():
                self.done[at.s] = self.summed[k]

            @pl.when(s_to != at.s)
            def _():
                remote(
                    self.summed.at[k],
                    self.done.at[at.s],
                    self.sem.at[3, 0],
                    self.sem.at[3, 1],
                    {"seq": s_to},
                ).start()

        each(0, at.S // 2, one)

    def total(self):
        at = self.at

        @pl.when(at.mine)
        def _():
            await_bytes(self.done.at[pl.ds(0, at.S - 1)], self.sem.at[3, 1])
            remote(
                self.done, self.done, self.sem.at[4, 0], self.sem.at[4, 1], at.flip()
            ).start()

    def finish(self):
        at = self.at
        each(0, at.F, lambda i: await_bytes(self.got.at[0], self.sem.at[0, i]))

        @pl.when(at.mine)
        def _():
            if at.S > 2:
                await_bytes(self.done.at[pl.ds(0, at.S // 2 - 1)], self.sem.at[3, 0])
            await_bytes(self.done, self.sem.at[4, 0])

        @pl.when(jnp.logical_not(at.mine))
        def _():
            await_bytes(self.summed, self.sem.at[3, 0])
            await_bytes(self.done, self.sem.at[4, 1])


class Tail:
    def __init__(self, at, mod_all, sums, first_in, mod_src, small_src, small_in, cond_src, cond_in, pieces, sem):
        self.at, self.sums, self.first_in = at, sums, first_in
        self.mod_src, self.mod_all = mod_src, mod_all
        self.small_src, self.small_in = small_src, small_in
        self.cond_src, self.cond_in, self.pieces, self.sem = cond_src, cond_in, pieces, sem

    @staticmethod
    def scratch(sizes, D, hidden, rows):
        R, F, S = sizes
        G = F * S
        C = D // S
        pack = 2 * D // G + 2 * rows + hidden // F
        wide = max(D, hidden, 3 * C)
        return [
            pltpu.VMEM((10, wide), F32),
            pltpu.VMEM((S, 10, wide), F32),
            pltpu.VMEM((6, D), BF),
            pltpu.VMEM((F, 1, pack), F32),
            pltpu.VMEM((R * F, 1, pack), F32),
            pltpu.VMEM((R * F, 1, rows), F32),
            pltpu.VMEM((G, 1, rows), F32),
            pltpu.VMEM((G, 1, pack), F32),
            DMA((8, max(S, 2 * F, G))),
        ]

    def first_copy(self, j):
        at = self.at
        return remote(
            self.sums, self.first_in.at[at.s], self.sem.at[0, j], self.sem.at[1, j], {"seq": at.ss(j)}
        )

    def start(self, mod_sums, b_one, b_two, b_out, b_qkv):
        sums = self.sums
        D = mod_sums.shape[1]
        hidden = b_one.shape[1]
        sums[...] = jnp.zeros_like(sums)
        sums[0:6, 0:D] = mod_sums[...]
        sums[6:7, 0:hidden] = b_one[...]
        sums[7:8, 0:D] = b_two[...]
        sums[8:9, 0:D] = b_out[...]
        sums[9:10, 0 : b_qkv.shape[1]] = b_qkv[...]
        each(1, self.at.S, lambda j: self.first_copy(j).start())
        self.first_in[self.at.s] = sums[...]

    def wide_copies(self, i):
        at = self.at
        slot = at.y * at.F + at.z
        device = {"rep": lax.rem(at.y + i // at.F, 2), "fsdp": at.zs(i)}
        return (
            remote(self.mod_src, self.mod_all.at[slot], self.sem.at[2, i], self.sem.at[3, i], device),
            remote(
                self.small_src.at[at.zs(i)],
                self.small_in.at[slot],
                self.sem.at[4, i],
                self.sem.at[5, i],
                device,
            ),
        )

    def middle(self, D, hidden, rows):
        at = self.at
        F, S, G = at.F, at.S, at.G
        C = D // S
        qv = 2 * D // G
        each(1, S, lambda j: self.first_copy(j).wait())
        total = self.first_in[0]
        for t in range(1, S):
            total = total + self.first_in[t]
        self.mod_src[...] = total[0:6, 0:D].astype(BF)
        for g in range(G):
            g_half = g % (G // 2)
            t = g_half // (F // 2)
            col = (g_half % (F // 2)) * qv + (2 * C if g >= G // 2 else 0)
            self.pieces[g, :, 0:qv] = self.first_in[t, 9:10, col : col + qv]
            self.pieces[g, :, qv : qv + rows] = total[8:9, g * rows : (g + 1) * rows]
            self.pieces[g, :, qv + rows : qv + 2 * rows] = total[7:8, g * rows : (g + 1) * rows]
        block = hidden // F
        for f in range(F):
            self.small_src[f, :, 0 : qv + 2 * rows] = self.pieces[f * S + at.s][:, 0 : qv + 2 * rows]
            self.small_src[f, :, qv + 2 * rows :] = self.sums[6:7, f * block : (f + 1) * block]

        def send(i):
            first, second = self.wide_copies(i)
            first.start()
            second.start()

        each(1, 2 * F, send)
        slot = at.y * F + at.z
        self.mod_all[slot] = self.mod_src[...]
        self.small_in[slot] = self.small_src[at.z]

    def cond_copy(self, i):
        at = self.at
        to = lax.rem(at.me + i, at.G)
        return remote(
            self.cond_src.at[at.y * at.F + to // at.S],
            self.cond_in.at[at.me],
            self.sem.at[6, i],
            self.sem.at[7, i],
            {"fsdp": to // at.S, "seq": lax.rem(to, at.S)},
        )

    def owners(self, w_ada, small_out):
        at = self.at
        F, G = at.F, at.G
        D = self.mod_src.shape[1]

        def arrive(i):
            first, second = self.wide_copies(i)
            first.wait()
            second.wait()

        each(1, 2 * F, arrive)
        cond = None
        for v in range(6):
            rows = self.mod_all[:, v, :]
            part = mm_nt(rows, w_ada[:, v * D : (v + 1) * D])
            cond = part if cond is None else cond + part
        for i in range(2 * F):
            self.cond_src[i] = cond[i : i + 1, :]
        each(1, G, lambda i: self.cond_copy(i).start())
        self.cond_in[at.me] = self.cond_src[at.y * F + at.z]
        total = self.small_in[0]
        for i in range(1, 2 * F):
            total = total + self.small_in[i]
        small_out[...] = total

    def finish(self, cond, grad_cond):
        at = self.at
        rows = self.cond_in.shape[2]
        each(1, at.G, lambda i: self.cond_copy(i).wait())
        for g in range(at.G):
            cols = slice(g * rows, (g + 1) * rows)
            value = cond[:, cols].astype(F32)
            gate = jax.nn.sigmoid(value)
            grad_cond[:, cols] = self.cond_in[g] * gate * (1.0 + value * (1.0 - gate))


def backward_kernel(sizes, *refs):
    at = Place(sizes)
    R, F, S, G = at.R, at.F, at.S, at.G
    grad_heads, heads, two_g, two_part, out_g, w_qkv, mixed_all, latents, grad_resid, w_ada = refs[-10:]
    log_sums, mod, sums_in, b_one, b_two, b_out, cond, one_g = refs[:8]
    given = refs[8:18]
    refs = refs[:7] + refs[8:]
    o_latents, o_qkv, o_one, o_two, o_part, o_out, o_mod, o_small, o_cond = refs[17:26]
    refs = refs[:16] + refs[17:]
    grad_in, key_flip, key_grad, val_grad, grad_proj, qkv_wide, qkv_g, mod_sums, b_qkv, in_sem = refs[25:35]
    rest = list(refs[35:])
    mix_sum = SeqSum(at, *rest[0:4])
    mix_src = rest[0]
    qkv = ColumnScatter(at, qkv_g, *rest[4:10], o_qkv, rest[10])
    one = ColumnScatter(at, one_g, *rest[11:17], o_one, rest[17])
    two = RowOwner(at, lambda z: two_g.at[z], rest[18], rest[19], rest[20])
    out = FullScatter(at, out_g, *rest[21:25], o_out, rest[25])
    tail = Tail(at, o_mod, *rest[26:35])
    load_sem, swap_sem, save_sem, grad_latents = rest[35:39]
    held = rest[39:49]
    two_swap = Swap(at, o_two, swap_sem.at[0])
    part_swap = Swap(at, o_part, swap_sem.at[1])
    saves = Moves(save_sem, (grad_latents, o_latents))
    loads = Moves(load_sem, *zip(given, held))
    loads.start()
    _, L, C = grad_heads.shape
    rows_own, D = o_out.shape[1:]
    hidden = one_g.shape[2]
    local_heads = H // S
    size = D // H
    greet(G, lambda i: {"fsdp": lax.rem(at.me + i, G) // S, "seq": lax.rem(at.me + i, S)})
    greet(2 * F, lambda i: {"rep": lax.rem(at.y + i // F, 2), "fsdp": at.zs(i)})
    loads.wait(0, 2, 3, 4)
    o_part[at.y] = two_part[...]
    greet_wait(G - 1 + 2 * F - 1)

    def in_copy(j):
        return remote(
            grad_heads.at[at.peer(j)],
            grad_in.at[at.s],
            in_sem.at[0, j],
            in_sem.at[1, j],
            {"seq": at.peer(j)},
        )

    each(1, S, lambda j: in_copy(j).start())
    one.start()
    two.start()
    out.start()
    grad_in[at.s] = grad_heads[at.s]
    key_grad[...] = jnp.zeros_like(key_grad)
    val_grad[...] = jnp.zeros_like(val_grad)
    loads.wait(1)
    for h in range(local_heads):
        key_flip[h] = heads[local_heads + h].T
    factor = size ** (-0.5) * log2e
    score_scale = size ** (-0.5)
    pad = jnp.zeros((L, LANES - size), BF)

    def block(j):
        t = at.peer(j)

        @pl.when(j > 0)
        def _():
            in_copy(j).wait()

        rows = pl.ds(pl.multiple_of(t * L, L), L)
        for h in range(local_heads):
            query = heads[h, rows, :]
            grad = jnp.concatenate([grad_in[t, :, h * size : (h + 1) * size], pad], axis=1)
            scores = mm_nt(heads[local_heads + h], query) * factor
            probs = jnp.exp2(scores - log_sums[h, t])
            grad_probs = mm_nt(heads[2 * local_heads + h], grad)
            inner = jnp.sum(probs * grad_probs, axis=0, keepdims=True)
            grad_scores = (probs * (grad_probs - inner)).astype(BF)
            query_grad = mm(key_flip[h], grad_scores) * score_scale
            grad_proj[t, :, h * size : (h + 1) * size] = query_grad.T[:, :size].astype(BF)
            key_grad[h] += mm(grad_scores, query)
            val_grad[h] += mm(probs.astype(BF), grad)

        pl.when(j == 0)(out.cross)

    each(0, S, block)
    two.relay()
    for h in range(local_heads):
        low = (key_grad[h] * score_scale)[:, :size].astype(BF)
        grad_proj[:, :, C + h * size : C + (h + 1) * size] = low.reshape(S, L, size)
        low = val_grad[h][:, :size].astype(BF)
        grad_proj[:, :, 2 * C + h * size : 2 * C + (h + 1) * size] = low.reshape(S, L, size)

    loads.wait(5, 6)

    def spread(index):
        t = at.peer(arrival(index))
        mix_src[t] = mm_nt(grad_proj[t], w_qkv[...]).astype(BF)
        mix_sum.send(index)

    grads = grad_proj[...].reshape(S * L, 3 * C)
    qkv_wide[...] = mm_tn(mixed_all[...].reshape(S * L, D), grads)
    for g in range(G):
        qkv_g[g] = qkv_wide[g * rows_own : (g + 1) * rows_own, :].astype(BF)
    qkv.start()
    out.scatter()
    each(0, S, lambda index: spread(lax.rem(index + 2, S)))
    one.scatter()
    b_qkv[...] = jnp.sum(grads.astype(F32), axis=0, keepdims=True)
    mix_sum.wait()
    loads.wait(7, 8, 9)
    step = min(32, L)
    mod_sums[...] = sums_in[...]
    scale = mod[1:2, :]

    def back(i):
        rows = pl.ds(pl.multiple_of(i * step, step), step)
        grad_mixed = mix_sum.total(rows)
        normed, inv_std = norm_stats(latents[rows, :].astype(F32))
        grad_latents[rows, :] = grad_resid[rows, :] + norm_back(
            grad_mixed * (1.0 + scale), normed, inv_std
        )
        mod_sums[0:1, :] += jnp.sum(grad_mixed, axis=0, keepdims=True)
        mod_sums[1:2, :] += jnp.sum(grad_mixed * normed, axis=0, keepdims=True)

    each(0, L // step, back)
    saves.start()
    tail.start(mod_sums, b_one, b_two, b_out, b_qkv)
    one.relay()
    tail.middle(D, hidden, rows_own)
    qkv.scatter()
    o_two[at.y] = two.total()
    two_swap.start()
    part_swap.start()
    out.total()
    one.near()
    qkv.relay()
    tail.owners(w_ada, o_small)
    one.total()
    qkv.near()
    tail.finish(cond, o_cond)
    qkv.total()
    out.finish()
    two_swap.finish()
    part_swap.finish()
    one.finish()
    qkv.finish()
    saves.wait()


def backward(sizes, *args):
    R, F, S = sizes
    G = F * S
    one_g, grad_heads, two_g = args[7], args[8], args[10]
    two_part, latents, w_ada = args[11], args[15], args[17]
    _, L, C = grad_heads.shape
    D = latents.shape[1]
    T = S * L
    local_heads = H // S
    rows = w_ada.shape[0]
    hidden = one_g.shape[2]
    pack = 2 * D // G + 2 * rows + hidden // F
    shape = jax.ShapeDtypeStruct
    return pl.pallas_call(
        lambda *refs: backward_kernel(sizes, *refs),
        name="backward",
        out_shape=(
            shape((L, D), F32),
            shape((S, rows, 3 * C), BF),
            shape((S, rows, hidden), BF),
            shape((2,) + two_g.shape[1:], BF),
            shape((2,) + two_part.shape, BF),
            shape((2, rows, D), BF),
            shape((R * F, 6, D), BF),
            shape((1, pack), F32),
            shape((1, D), F32),
        ),
        in_specs=[VM] * 7 + [HB] * 11,
        out_specs=(HB,) + (VM,) * 8,
        scratch_shapes=[
            pltpu.VMEM((S, L, C), BF),
            pltpu.VMEM((local_heads, LANES, T), BF),
            pltpu.VMEM((local_heads, T, LANES), F32),
            pltpu.VMEM((local_heads, T, LANES), F32),
            pltpu.VMEM((S, L, 3 * C), BF),
            pltpu.VMEM((D, 3 * C), F32),
            pltpu.VMEM((G, rows, 3 * C), BF),
            pltpu.VMEM((6, D), F32),
            pltpu.VMEM((1, 3 * C), F32),
            DMA((2, S)),
        ]
        + SeqSum.scratch(S, L, D)
        + ColumnScatter.scratch(sizes, rows, 3 * C)
        + ColumnScatter.scratch(sizes, rows, hidden)
        + RowOwner.scratch(F, two_g.shape[1:])
        + FullScatter.scratch(sizes, rows, D)
        + Tail.scratch(sizes, D, hidden, rows)
        + [DMA((10,)), DMA((2, 2)), DMA((1,)), pltpu.VMEM((L, D), F32)]
        + [pltpu.VMEM(x.shape, x.dtype) for x in args[8:]],
        compiler_params=params(4, 60),
    )(*args)


def assemble_kernel(sizes, *refs):
    R, F, S = sizes
    G = F * S
    n = 11
    given, results = refs[:n], refs[n : n + 13]
    qkv, one, two, part, out, mod_all, silu_all, small = refs[n + 13 : n + 21]
    o_qkv, o_one, o_two, o_out, o_ada, b_ada, b_qv, b_out, b_one, b_two = refs[n + 21 : n + 31]
    flat, pieces, load_sem, save_sem, *passing = refs[n + 31 :]
    held = (qkv, one, two, part, out, mod_all, silu_all, small, *passing)
    loads = Moves(load_sem, *zip(given, held))
    loads.start()
    passed = tuple(zip(passing, results[:3]))
    made = (o_ada, b_ada, o_qkv, b_qv, o_out, b_out, o_one, b_one, o_two, b_two)
    saves = Moves(save_sem, *passed, *zip(made, results[3:]))
    rows, D = o_out.shape
    C = D // S
    hidden = one.shape[2]
    block = hidden // F
    loads.wait(5, 6)
    silu = silu_all[:, 0, :].astype(BF)
    width = b_ada.shape[1]
    for v in range(6):
        grads = mod_all[:, v, :]
        o_ada[:, v * D : (v + 1) * D] = mm_tn(silu, grads)
        flat[:, v * D : (v + 1) * D] = jnp.sum(grads.astype(F32), axis=0, keepdims=True)
    saves.start(3)
    for g in range(G):
        pieces[g] = flat[:, g * width : (g + 1) * width]
    b_ada[...] = pieces[lax.axis_index("fsdp") * S + lax.axis_index("seq")]
    loads.wait(7)
    first = b_qv.shape[1]
    b_qv[...] = small[:, :first]
    b_out[...] = small[:, first : first + rows]
    b_two[...] = small[:, first + rows : first + 2 * rows]
    b_one[...] = small[:, first + 2 * rows :]
    saves.start(4, 6, 8, 10, 12)
    loads.wait(1)
    for t in range(S):
        for f in range(F):
            col = (f * S + t) * block
            o_one[:, col : col + block] = one[t, :, f * block : (f + 1) * block].astype(F32)
    saves.start(9)
    loads.wait(2, 3)
    o_two[0:2] = part[0].astype(F32) + part[1].astype(F32)
    o_two[2:4] = two[...].astype(F32)
    saves.start(11)
    loads.wait(0)
    for t in range(S):
        for j in range(3):
            o_qkv[:, j * D + t * C : j * D + (t + 1) * C] = qkv[t, :, j * C : (j + 1) * C].astype(F32)
    saves.start(5)
    loads.wait(4, 8, 9, 10)
    saves.start(0, 1, 2)
    o_out[...] = out[0].astype(F32) + out[1].astype(F32)
    saves.start(7)
    saves.wait()


def assemble(sizes, qkv, one, two, part, out, mod_all, silu_all, small, *passed):
    R, F, S = sizes
    G = F * S
    rows, D = out.shape[1:]
    hidden = one.shape[2]
    made = (
        ((rows, 6 * D), F32),
        ((1, 6 * D // G), F32),
        ((rows, 3 * D), F32),
        ((1, 2 * D // G), F32),
        ((rows, D), F32),
        ((1, rows), F32),
        ((rows, hidden * S), F32),
        ((1, hidden // F), F32),
        ((4,) + two.shape[1:], F32),
        ((1, rows), F32),
    )
    given = (qkv, one, two, part, out, mod_all, silu_all, small)
    scratch = [pltpu.VMEM(x.shape, x.dtype) for x in given]
    order = (2, 6, 8, 4, 0, 1, 3, 5, 7, 9)
    return pl.pallas_call(
        lambda *refs: assemble_kernel(sizes, *refs),
        name="assemble",
        out_shape=tuple(jax.ShapeDtypeStruct(x.shape, x.dtype) for x in passed)
        + tuple(jax.ShapeDtypeStruct(*item) for item in made),
        in_specs=[HB] * 11,
        out_specs=(HB,) * 13,
        scratch_shapes=scratch
        + [pltpu.VMEM(*made[i]) for i in order]
        + [
            pltpu.VMEM((1, 6 * D), F32),
            pltpu.VMEM((G, 1, 6 * D // G), F32),
            DMA((11,)),
            DMA((13,)),
        ]
        + [pltpu.VMEM(x.shape, x.dtype) for x in passed],
        compiler_params=pltpu.CompilerParams(vmem_limit_bytes=60 * 1024 * 1024),
    )(*given, *passed)


def on_device(
    latents, cond, w_ada, b_ada, w_qkv, b_qv, w_out, b_out, w_one, b_one, w_two, b_two, cotangent
):
    sizes = R, F, S = tuple(lax.axis_size(name) for name in ("rep", "fsdp", "seq"))
    G = F * S
    _, L, D = latents.shape
    hidden = w_one.shape[1] // S
    rows = w_ada.shape[0]
    tokens = latents[0]
    two_rows = w_two.shape[0]
    (
        mixed_all,
        heads,
        merged,
        branch_one,
        mix_all,
        grad_all,
        full_qkv,
        full_out,
        log_sums,
        mod,
        silu_all,
        bias_one,
        bias_two,
        g_one,
        g_two,
    ) = forward(
        sizes,
        cond,
        jnp.concatenate([b.astype(F32) for b in (b_ada, b_qv, b_out, b_two, b_one)])[None],
        tokens,
        cotangent[0],
        w_ada,
        w_qkv,
        w_one,
        w_two.reshape(2, two_rows // 2, D),
        w_out,
    )
    full_one = g_one.reshape(D, hidden)
    full_two = g_two.reshape(hidden, D)
    (
        block_out,
        grad_resid,
        grad_heads,
        one_g,
        two_g,
        two_part,
        out_g,
        grad_b_one,
        grad_b_two,
        grad_b_out,
        mod_sums,
    ) = mlp(
        sizes,
        mod,
        bias_one,
        bias_two,
        full_one,
        mix_all,
        full_two,
        grad_all,
        tokens,
        branch_one,
        cotangent[0],
        full_out,
        merged,
    )
    grad_latents, qkv_sum, one_sum, two_sum, part_sum, out_sum, mod_all, o_small, o_cond = backward(
        sizes,
        log_sums,
        mod,
        mod_sums,
        grad_b_one,
        grad_b_two,
        grad_b_out,
        cond,
        one_g.reshape(G, rows, hidden),
        grad_heads,
        heads,
        two_g,
        two_part,
        out_g,
        full_qkv,
        mixed_all,
        tokens,
        grad_resid,
        w_ada,
    )
    outs = assemble(
        sizes,
        qkv_sum,
        one_sum,
        two_sum,
        part_sum,
        out_sum,
        mod_all,
        silu_all,
        o_small,
        block_out,
        grad_latents,
        o_cond,
    )
    shapes = (latents.shape, latents.shape, cond.shape, w_ada.shape, b_ada.shape, w_qkv.shape, b_qv.shape)
    shapes += (w_out.shape, b_out.shape, w_one.shape, b_one.shape, w_two.shape, b_two.shape)
    return tuple(out.reshape(want) for out, want in zip(outs, shapes))


def solution(mesh):
    owned = P(("fsdp", "seq"), None)
    owned_bias = P(("fsdp", "seq"))
    token_spec = P(("rep", "fsdp"), "seq", None)
    cond_spec = P(("rep", "fsdp"), None)
    weights = (owned, owned_bias) * 5
    in_specs = (token_spec, cond_spec) + weights + (token_spec,)
    out_specs = (token_spec, token_spec, cond_spec) + weights
    return jax.shard_map(
        on_device, mesh=mesh, in_specs=in_specs, out_specs=out_specs, check_vma=False
    )
```

profile of v0, /device:TPU:0, one launch (start us, length us, event | category | flops | bytes accessed | tf_op | source)
XLA Modules:
  0.0 273.7 jit_solution(15500550807756475615)
XLA Ops:
  0.6 3.5 %concatenate.4 = bf16[1008]{0:T(1024)(128)(2,1)S(1)} concatenate(bf16[432]{0:T(512)(128)(2,1)} %param.16, bf16[144]{0:T(256)(128)(2,1)} %param.18, bf16[72]{0:T(256)(128)(2,1)} %param.20, bf16[72]{0:T(256)(128)(2,1)} %param.24, bf16[288]{0:T(512)(128)(2,1)} %param.22), dimensions={0} | concatenate | bytes 4032 | tf_op jit(solution)/shard_map/concatenate | solution.py:1824
  4.1 0.6 broadcast_in_dim.7
  4.7 115.9 %forward.1 = (bf16[4,256,1152]{2,1,0:T(8,128)(2,1)}, bf16[12,1024,128]{2,1,0:T(8,128)(2,1)}, bf16[256,1152]{1,0:T(8,128)(2,1)}, f32[256,1152]{1,0:T(8,128)}, bf1...) custom-call(bf16[1,1152]{1,0:T(2,128)(2,1)} %refs_6_.3, ...), custom_call_target="tpu_custom_call" | custom-call | tf_op jit(solution)/shard_map/forward/pallas_call | solution.py:751
  120.6 43.7 %mlp.1 = (bf16[256,1152]{1,0:T(8,128)(2,1)}, f32[256,1152]{1,0:T(8,128)}, bf16[4,256,288]{2,1,0:T(8,128)(2,1)}, bf16[1152,1152]{1,0:T(8,128)(2,1)}, bf16[4,72,11...) custom-call(f32[6,1152]{1,0:T(8,128)} %get-tuple-element.62.refs_0_., ...), custom_call_target="tpu_custom_call" | custom-call | tf_op jit(solution)/shard_map/mlp/pallas_call | solution.py:1219
  164.3 102.6 %backward.1 = (f32[256,1152]{1,0:T(8,128)}, bf16[4,72,864]{2,1,0:T(8,128)(2,1)}, bf16[4,72,1152]{2,1,0:T(8,128)(2,1)}, bf16[2,72,1152]{2,1,0:T(8,128)(2,1)}, bf1...) custom-call(f32[4,4,1,256]{3,2,1,0:T(1,128)} %get-tuple-element.61.r, ...), custom_call_target="tpu_custom_call" | custom-call | tf_op jit(solution)/shard_map/backward/pallas_call | solution.py:1657
  266.9 5.6 %assemble.1 = (bf16[256,1152]{1,0:T(8,128)(2,1)}, f32[256,1152]{1,0:T(8,128)}, f32[1,1152]{1,0:T(1,128)}, f32[72,6912]{1,0:T(8,128)}, f32[1,432]{1,0:T(1,128)}, ...) custom-call(bf16[4,72,864]{2,1,0:T(8,128)(2,1)} %get-tuple-element.8, ...), custom_call_target="tpu_custom_call" | custom-call | tf_op jit(solution)/shard_map/assemble/pallas_call | solution.py:1775
  272.4 1.3 reduce
where the time goes:
time: 274 us
  Pallas kernels  268 us (98%)
  local copies, waits for them, and re-layouts  3.47 us (1%)
    pallas_call x1, Pallas kernels, forward(): pl.pallas_call(lambda *refs: forward_kernel(sizes, *refs), name='forward'...  116 us
    pallas_call x1, Pallas kernels, backward(): pl.pallas_call(lambda *refs: backward_kernel(sizes, *refs), name='backwar...  103 us
    pallas_call x1, Pallas kernels, mlp(): pl.pallas_call(lambda *refs: mlp_kernel(sizes, *refs), name='mlp', out_sh...  43.7 us
    pallas_call x1, Pallas kernels, assemble(): pl.pallas_call(lambda *refs: assemble_kernel(sizes, *refs), name='assembl...  5.57 us

commit v1 on v0

--- a/solution.py
+++ b/solution.py
@@ -441,16 +441,20 @@
 def forward_kernel(sizes, *refs):
     at = Place(sizes)
     R, F, S, G = at.R, at.F, at.S, at.G
-    cond, biases = refs[:2]
-    i_latents, i_cotangent, i_ada, i_qkv, i_one, w_two, w_out = refs[2:9]
-    refs = refs[:1] + refs
+    cond = refs[0]
+    i_biases = refs[1:6]
+    i_latents, i_cotangent, i_ada, i_qkv, i_one, w_two, w_out = refs[6:13]
+    refs = refs[3:]
     o_mixed, o_heads, o_merged, o_branch, o_mix, o_grad, o_full_qkv, o_full_out = refs[10:18]
     log_sums, mod, silu_all, bias_one, bias_two, g_one, g_two = refs[18:25]
     silu_src, part, parts_in, mod_src, mod_in, qkv_src, one_src, pack_all = refs[25:33]
     g_qkv, g_out, wide, bias_qkv, bias_out, val_flip, att, merged_in = refs[33:41]
     silu_sem, part_sem, mod_sem, pack_sem, qkv_sem, one_sem, two_sem, out_sem = refs[41:49]
     mixed_sem, grad_sem, att_sem, mix_sem, spread_sem, load_sem, save_sem = refs[49:56]
-    bias_pack, bias_pieces, bias_slot = refs[69:72]
+    bias_pack, bias_pieces, bias_slot, bias_sem = refs[69:73]
+    biases = refs[73:78]
+    bias_loads = Moves(bias_sem, *zip(i_biases, biases))
+    bias_loads.start()
     latents, cotangent, w_ada, w_qkv, w_one = refs[56:61]
     mixed_all, heads, merged, branch_one, mix_all, grad_all, full_qkv, full_out = refs[61:69]
     loads = Moves(
@@ -484,9 +488,14 @@
     greet(G, lambda i: {"fsdp": lax.rem(at.me + i, G) // S, "seq": lax.rem(at.me + i, S)})
     greet(2 * F, lambda i: {"rep": lax.rem(at.y + i // F, 2), "fsdp": at.zs(i)})
     width = bias_pieces.shape[2]
-    bias_pack[...] = biases[:, width:].astype(F32)
+    bias_loads.wait()
+    first = 0
+    for bias in biases[1:]:
+        length = bias.shape[0]
+        bias_pack[:, first : first + length] = bias[...].astype(F32).reshape(1, length)
+        first = first + length
     bias_pieces[...] = jnp.zeros_like(bias_pieces)
-    bias_pieces[at.me] = biases[:, :width].astype(F32)
+    bias_pieces[at.me] = biases[0][...].astype(F32).reshape(1, width)
     for g in range(G):
         bias_slot[:, g * width : (g + 1) * width] = bias_pieces[g]
 
@@ -726,7 +735,9 @@
     saves.wait()
 
 
-def forward(sizes, cond, biases, latents, cotangent, w_ada, w_qkv, w_one, w_two, w_out):
+def forward(sizes, cond, *args):
+    biases = args[:5]
+    latents, cotangent, w_ada, w_qkv, w_one, w_two, w_out = args[5:]
     R, F, S = sizes
     G = F * S
     rows, D = w_out.shape
@@ -737,7 +748,7 @@
     hidden = w_one.shape[1] // S
     shape = jax.ShapeDtypeStruct
     width = 6 * D // G
-    pack = biases.shape[1] - width
+    pack = sum(bias.shape[0] for bias in biases[1:])
     kept = (
         ((S, L, D), BF),
         ((3 * local_heads, T, LANES), BF),
@@ -761,7 +772,7 @@
             shape((G, rows, hidden), BF),
             shape((F,) + w_two.shape, BF),
         ),
-        in_specs=[VM] * 2 + [HB] * 7,
+        in_specs=[VM] + [HB] * 12,
         out_specs=(HB,) * 8 + (VM,) * 5 + (HB,) * 2,
         scratch_shapes=[
             pltpu.VMEM((G, 1, rows), F32),
@@ -802,9 +813,11 @@
             pltpu.VMEM((1, pack), F32),
             pltpu.VMEM((G, 1, width), F32),
             pltpu.VMEM((1, 6 * D), F32),
-        ],
+            DMA((5,)),
+        ]
+        + [pltpu.VMEM(bias.shape, BF) for bias in biases],
         compiler_params=params(1, 60),
-    )(cond, biases, latents, cotangent, w_ada, w_qkv, w_one, w_two, w_out)
+    )(cond, *args)
 
 
 class RowScatter:
@@ -1501,22 +1514,25 @@
     log_sums, mod, sums_in, b_one, b_two, b_out, cond, one_g = refs[:8]
     given = refs[8:18]
     refs = refs[:7] + refs[8:]
-    o_latents, o_qkv, o_one, o_two, o_part, o_out, o_mod, o_small, o_cond = refs[17:26]
+    targets = refs[17:24]
+    o_small, o_cond = refs[24:26]
     refs = refs[:16] + refs[17:]
     grad_in, key_flip, key_grad, val_grad, grad_proj, qkv_wide, qkv_g, mod_sums, b_qkv, in_sem = refs[25:35]
     rest = list(refs[35:])
     mix_sum = SeqSum(at, *rest[0:4])
     mix_src = rest[0]
+    load_sem, swap_sem, save_sem = rest[35:38]
+    kept = rest[38:45]
+    grad_latents, o_qkv, o_one, o_two, o_part, o_out, o_mod = kept
+    held = rest[45:55]
     qkv = ColumnScatter(at, qkv_g, *rest[4:10], o_qkv, rest[10])
     one = ColumnScatter(at, one_g, *rest[11:17], o_one, rest[17])
     two = RowOwner(at, lambda z: two_g.at[z], rest[18], rest[19], rest[20])
     out = FullScatter(at, out_g, *rest[21:25], o_out, rest[25])
     tail = Tail(at, o_mod, *rest[26:35])
-    load_sem, swap_sem, save_sem, grad_latents = rest[35:39]
-    held = rest[39:49]
     two_swap = Swap(at, o_two, swap_sem.at[0])
     part_swap = Swap(at, o_part, swap_sem.at[1])
-    saves = Moves(save_sem, (grad_latents, o_latents))
+    saves = Moves(save_sem, *zip(kept, targets))
     loads = Moves(load_sem, *zip(given, held))
     loads.start()
     _, L, C = grad_heads.shape
@@ -1617,7 +1633,7 @@
         mod_sums[1:2, :] += jnp.sum(grad_mixed * normed, axis=0, keepdims=True)
 
     each(0, L // step, back)
-    saves.start()
+    saves.start(0)
     tail.start(mod_sums, b_one, b_two, b_out, b_qkv)
     one.relay()
     tail.middle(D, hidden, rows_own)
@@ -1629,15 +1645,20 @@
     one.near()
     qkv.relay()
     tail.owners(w_ada, o_small)
+    saves.start(6)
     one.total()
     qkv.near()
     tail.finish(cond, o_cond)
     qkv.total()
-    out.finish()
     two_swap.finish()
     part_swap.finish()
+    saves.start(3, 4)
+    out.finish()
+    saves.start(5)
     one.finish()
+    saves.start(2)
     qkv.finish()
+    saves.start(1)
     saves.wait()
 
 
@@ -1654,22 +1675,25 @@
     hidden = one_g.shape[2]
     pack = 2 * D // G + 2 * rows + hidden // F
     shape = jax.ShapeDtypeStruct
+    kept = (
+        ((L, D), F32),
+        ((S, rows, 3 * C), BF),
+        ((S, rows, hidden), BF),
+        ((2,) + two_g.shape[1:], BF),
+        ((2,) + two_part.shape, BF),
+        ((2, rows, D), BF),
+        ((R * F, 6, D), BF),
+    )
     return pl.pallas_call(
         lambda *refs: backward_kernel(sizes, *refs),
         name="backward",
-        out_shape=(
-            shape((L, D), F32),
-            shape((S, rows, 3 * C), BF),
-            shape((S, rows, hidden), BF),
-            shape((2,) + two_g.shape[1:], BF),
-            shape((2,) + two_part.shape, BF),
-            shape((2, rows, D), BF),
-            shape((R * F, 6, D), BF),
+        out_shape=tuple(shape(*item) for item in kept)
+        + (
             shape((1, pack), F32),
             shape((1, D), F32),
         ),
         in_specs=[VM] * 7 + [HB] * 11,
-        out_specs=(HB,) + (VM,) * 8,
+        out_specs=(HB,) * 7 + (VM,) * 2,
         scratch_shapes=[
             pltpu.VMEM((S, L, C), BF),
             pltpu.VMEM((local_heads, LANES, T), BF),
@@ -1688,7 +1712,8 @@
         + RowOwner.scratch(F, two_g.shape[1:])
         + FullScatter.scratch(sizes, rows, D)
         + Tail.scratch(sizes, D, hidden, rows)
-        + [DMA((10,)), DMA((2, 2)), DMA((1,)), pltpu.VMEM((L, D), F32)]
+        + [DMA((10,)), DMA((2, 2)), DMA((7,))]
+        + [pltpu.VMEM(*item) for item in kept]
         + [pltpu.VMEM(x.shape, x.dtype) for x in args[8:]],
         compiler_params=params(4, 60),
     )(*args)
@@ -1714,7 +1739,7 @@
     block = hidden // F
     loads.wait(5, 6)
     silu = silu_all[:, 0, :].astype(BF)
-    width = b_ada.shape[1]
+    width = b_ada.shape[0]
     for v in range(6):
         grads = mod_all[:, v, :]
         o_ada[:, v * D : (v + 1) * D] = mm_tn(silu, grads)
@@ -1722,13 +1747,13 @@
     saves.start(3)
     for g in range(G):
         pieces[g] = flat[:, g * width : (g + 1) * width]
-    b_ada[...] = pieces[lax.axis_index("fsdp") * S + lax.axis_index("seq")]
+    b_ada[...] = pieces[lax.axis_index("fsdp") * S + lax.axis_index("seq")].reshape(width)
     loads.wait(7)
-    first = b_qv.shape[1]
-    b_qv[...] = small[:, :first]
-    b_out[...] = small[:, first : first + rows]
-    b_two[...] = small[:, first + rows : first + 2 * rows]
-    b_one[...] = small[:, first + 2 * rows :]
+    first = 0
+    for bias in (b_qv, b_out, b_two, b_one):
+        length = bias.shape[0]
+        bias[...] = small[:, first : first + length].reshape(length)
+        first = first + length
     saves.start(4, 6, 8, 10, 12)
     loads.wait(1)
     for t in range(S):
@@ -1759,15 +1784,15 @@
     hidden = one.shape[2]
     made = (
         ((rows, 6 * D), F32),
-        ((1, 6 * D // G), F32),
+        ((6 * D // G,), F32),
         ((rows, 3 * D), F32),
-        ((1, 2 * D // G), F32),
+        ((2 * D // G,), F32),
         ((rows, D), F32),
-        ((1, rows), F32),
+        ((rows,), F32),
         ((rows, hidden * S), F32),
-        ((1, hidden // F), F32),
+        ((hidden // F,), F32),
         ((4,) + two.shape[1:], F32),
-        ((1, rows), F32),
+        ((rows,), F32),
     )
     given = (qkv, one, two, part, out, mod_all, silu_all, small)
     scratch = [pltpu.VMEM(x.shape, x.dtype) for x in given]
@@ -1821,7 +1846,11 @@
     ) = forward(
         sizes,
         cond,
-        jnp.concatenate([b.astype(F32) for b in (b_ada, b_qv, b_out, b_two, b_one)])[None],
+        b_ada,
+        b_qv,
+        b_out,
+        b_two,
+        b_one,
         tokens,
         cotangent[0],
         w_ada,

time: 274 us -> 269 us (0.982)
  local copies, waits for them, and re-layouts: 3.47 us -> 0 us
    concatenate x1 -> x0, local copies, waits for them, and re-layouts: 3.47 us -> none  [on_device(): jnp.concatenate([b.astype(F32) for b in (b_ada, b_qv, b_out, b_two, b_one)])]
where the time goes in v1:
time: 269 us; the launch traced here: 268 us
  Pallas kernels  268 us (100%)
    pallas_call x1, Pallas kernels, forward(): pl.pallas_call(lambda *refs: forward_kernel(sizes, *refs), name='forward'...  116 us
    pallas_call x1, Pallas kernels, backward(): pl.pallas_call(lambda *refs: backward_kernel(sizes, *refs), name='backwar...  102 us
    pallas_call x1, Pallas kernels, mlp(): pl.pallas_call(lambda *refs: mlp_kernel(sizes, *refs), name='mlp', out_sh...  43.4 us
    pallas_call x1, Pallas kernels, assemble(): pl.pallas_call(lambda *refs: assemble_kernel(sizes, *refs), name='assembl...  5.56 us

profile of v1, /device:TPU:0, one launch (start us, length us, event | category | flops | bytes accessed | tf_op | source)
XLA Modules:
  0.0 268.5 jit_solution(11431351787411218222)
XLA Ops:
  0.6 116.1 %forward.1 = (bf16[4,256,1152]{2,1,0:T(8,128)(2,1)}, bf16[12,1024,128]{2,1,0:T(8,128)(2,1)}, bf16[256,1152]{1,0:T(8,128)(2,1)}, f32[256,1152]{1,0:T(8,128)}, bf1...) custom-call(bf16[1,1152]{1,0:T(2,128)(2,1)} %refs_6_.1, ...), custom_call_target="tpu_custom_call" | custom-call | tf_op jit(solution)/shard_map/forward/pallas_call | solution.py:762
  116.8 43.4 %mlp.1 = (bf16[256,1152]{1,0:T(8,128)(2,1)}, f32[256,1152]{1,0:T(8,128)}, bf16[4,256,288]{2,1,0:T(8,128)(2,1)}, bf16[1152,1152]{1,0:T(8,128)(2,1)}, bf16[4,72,11...) custom-call(f32[6,1152]{1,0:T(8,128)} %get-tuple-element.62.refs_0_., ...), custom_call_target="tpu_custom_call" | custom-call | tf_op jit(solution)/shard_map/mlp/pallas_call | solution.py:1232
  160.3 102.5 %backward.1 = (f32[256,1152]{1,0:T(8,128)}, bf16[4,72,864]{2,1,0:T(8,128)(2,1)}, bf16[4,72,1152]{2,1,0:T(8,128)(2,1)}, bf16[2,72,1152]{2,1,0:T(8,128)(2,1)}, bf1...) custom-call(f32[4,4,1,256]{3,2,1,0:T(1,128)} %get-tuple-element.61.r, ...), custom_call_target="tpu_custom_call" | custom-call | tf_op jit(solution)/shard_map/backward/pallas_call | solution.py:1687
  262.7 5.6 %assemble.1 = (bf16[256,1152]{1,0:T(8,128)(2,1)}, f32[256,1152]{1,0:T(8,128)}, f32[1,1152]{1,0:T(1,128)}, f32[72,6912]{1,0:T(8,128)}, f32[432]{0:T(512)}, /*inde...) custom-call(bf16[4,72,864]{2,1,0:T(8,128)(2,1)} %get-tuple-element.8, ...), custom_call_target="tpu_custom_call" | custom-call | tf_op jit(solution)/shard_map/assemble/pallas_call | solution.py:1800

commit v2 on v1

--- a/solution.py
+++ b/solution.py
@@ -951,20 +951,23 @@
 
 
 class FullScatter:
-    def __init__(self, at, src, near, got, stage, inn, done, sem):
+    def __init__(self, at, src, near, got, stage, inn, far, along_sem, done, sem):
         self.at, self.src, self.near, self.got, self.stage = at, src, near, got, stage
-        self.inn, self.done, self.sem = inn, done, sem
+        self.done, self.sem = done, sem
+        self.along = RowOwner(at, lambda z: stage.at[z], inn, far, along_sem)
 
     @staticmethod
     def scratch(sizes, rows, cols):
         R, F, S = sizes
-        return [
-            pltpu.VMEM((S // 2, F, rows, cols), BF),
-            pltpu.VMEM((S // 2, F, rows, cols), BF),
-            pltpu.VMEM((F, rows, cols), BF),
-            pltpu.VMEM((F, rows, cols), BF),
-            DMA((10, max(F, S))),
-        ]
+        return (
+            [
+                pltpu.VMEM((S // 2, F, rows, cols), BF),
+                pltpu.VMEM((S // 2, F, rows, cols), BF),
+                pltpu.VMEM((F, rows, cols), BF),
+            ]
+            + RowOwner.scratch(F, (rows, cols))
+            + [DMA((6, max(F, S)))]
+        )
 
     def sibling(self, j):
         at = self.at
@@ -1005,16 +1008,6 @@
             self.direct(j).start()
         self.sibling(1).wait()
 
-    def out_copy(self, i):
-        at = self.at
-        return remote(
-            self.stage.at[at.zs(i)],
-            self.inn.at[at.z],
-            self.sem.at[4, i],
-            self.sem.at[5, i],
-            {"fsdp": at.zs(i)},
-        )
-
     def scatter(self):
         at = self.at
         for j in range(2, at.S, 2):
@@ -1027,26 +1020,18 @@
                 total = total + self.got[k, z_to].astype(F32)
             self.stage[z_to] = total.astype(BF)
 
-            @pl.when(i > 0)
-            def _():
-                self.out_copy(i).start()
-
         each(0, at.F, far)
-        self.inn[at.z] = self.stage[at.z]
+        self.along.start()
 
     def total(self):
         at = self.at
-        each(1, at.F, lambda i: self.out_copy(i).wait())
-        total = self.inn[0].astype(F32)
-        for f in range(1, at.F):
-            total = total + self.inn[f].astype(F32)
-        self.done[at.y] = total.astype(BF)
+        self.done[at.y] = self.along.total()
         mine = self.done.at[at.y]
-        remote(mine, mine, self.sem.at[6, 0], self.sem.at[7, 0], at.flip()).start()
+        remote(mine, mine, self.sem.at[4, 0], self.sem.at[5, 0], at.flip()).start()
 
     def finish(self):
-        await_bytes(self.done.at[0], self.sem.at[6, 0])
-        await_bytes(self.done.at[0], self.sem.at[7, 0])
+        await_bytes(self.done.at[0], self.sem.at[4, 0])
+        await_bytes(self.done.at[0], self.sem.at[5, 0])
 
 
 def mlp_kernel(sizes, *refs):
@@ -1521,15 +1506,15 @@
     rest = list(refs[35:])
     mix_sum = SeqSum(at, *rest[0:4])
     mix_src = rest[0]
-    load_sem, swap_sem, save_sem = rest[35:38]
-    kept = rest[38:45]
+    load_sem, swap_sem, save_sem = rest[37:40]
+    kept = rest[40:47]
     grad_latents, o_qkv, o_one, o_two, o_part, o_out, o_mod = kept
-    held = rest[45:55]
+    held = rest[47:57]
     qkv = ColumnScatter(at, qkv_g, *rest[4:10], o_qkv, rest[10])
     one = ColumnScatter(at, one_g, *rest[11:17], o_one, rest[17])
     two = RowOwner(at, lambda z: two_g.at[z], rest[18], rest[19], rest[20])
-    out = FullScatter(at, out_g, *rest[21:25], o_out, rest[25])
-    tail = Tail(at, o_mod, *rest[26:35])
+    out = FullScatter(at, out_g, *rest[21:27], o_out, rest[27])
+    tail = Tail(at, o_mod, *rest[28:37])
     two_swap = Swap(at, o_two, swap_sem.at[0])
     part_swap = Swap(at, o_part, swap_sem.at[1])
     saves = Moves(save_sem, *zip(kept, targets))
@@ -1616,6 +1601,8 @@
     each(0, S, lambda index: spread(lax.rem(index + 2, S)))
     one.scatter()
     b_qkv[...] = jnp.sum(grads.astype(F32), axis=0, keepdims=True)
+    out.along.relay()
+    one.relay()
     mix_sum.wait()
     loads.wait(7, 8, 9)
     step = min(32, L)
@@ -1635,7 +1622,6 @@
     each(0, L // step, back)
     saves.start(0)
     tail.start(mod_sums, b_one, b_two, b_out, b_qkv)
-    one.relay()
     tail.middle(D, hidden, rows_own)
     qkv.scatter()
     o_two[at.y] = two.total()

time: 269 us -> 266 us (0.989)
  Pallas kernels: 268 us -> 265 us
    pallas_call x1, Pallas kernels: 102 us -> 99.5 us  [backward(): pl.pallas_call(lambda *refs: backward_kernel(sizes, *refs), name='backwar...]
where the time goes in v2:
time: 266 us
  Pallas kernels  265 us (100%)
    pallas_call x1, Pallas kernels, forward(): pl.pallas_call(lambda *refs: forward_kernel(sizes, *refs), name='forward'...  116 us
    pallas_call x1, Pallas kernels, backward(): pl.pallas_call(lambda *refs: backward_kernel(sizes, *refs), name='backwar...  99.5 us
    pallas_call x1, Pallas kernels, mlp(): pl.pallas_call(lambda *refs: mlp_kernel(sizes, *refs), name='mlp', out_sh...  43.4 us
    pallas_call x1, Pallas kernels, assemble(): pl.pallas_call(lambda *refs: assemble_kernel(sizes, *refs), name='assembl...  5.56 us

profile of v2, /device:TPU:0, one launch (start us, length us, event | category | flops | bytes accessed | tf_op | source)
XLA Modules:
  0.0 265.5 jit_solution(13781626837535770305)
XLA Ops:
  0.6 116.1 %forward.1 = (bf16[4,256,1152]{2,1,0:T(8,128)(2,1)}, bf16[12,1024,128]{2,1,0:T(8,128)(2,1)}, bf16[256,1152]{1,0:T(8,128)(2,1)}, f32[256,1152]{1,0:T(8,128)}, bf1...) custom-call(bf16[1,1152]{1,0:T(2,128)(2,1)} %refs_6_.1, ...), custom_call_target="tpu_custom_call" | custom-call | tf_op jit(solution)/shard_map/forward/pallas_call | solution.py:762
  116.8 43.4 %mlp.1 = (bf16[256,1152]{1,0:T(8,128)(2,1)}, f32[256,1152]{1,0:T(8,128)}, bf16[4,256,288]{2,1,0:T(8,128)(2,1)}, bf16[1152,1152]{1,0:T(8,128)(2,1)}, bf16[4,72,11...) custom-call(f32[6,1152]{1,0:T(8,128)} %get-tuple-element.62.refs_0_., ...), custom_call_target="tpu_custom_call" | custom-call | tf_op jit(solution)/shard_map/mlp/pallas_call | solution.py:1217
  160.3 99.5 %backward.1 = (f32[256,1152]{1,0:T(8,128)}, bf16[4,72,864]{2,1,0:T(8,128)(2,1)}, bf16[4,72,1152]{2,1,0:T(8,128)(2,1)}, bf16[2,72,1152]{2,1,0:T(8,128)(2,1)}, bf1...) custom-call(f32[4,4,1,256]{3,2,1,0:T(1,128)} %get-tuple-element.61.r, ...), custom_call_target="tpu_custom_call" | custom-call | tf_op jit(solution)/shard_map/backward/pallas_call | solution.py:1673
  259.8 5.6 %assemble.1 = (bf16[256,1152]{1,0:T(8,128)(2,1)}, f32[256,1152]{1,0:T(8,128)}, f32[1,1152]{1,0:T(1,128)}, f32[72,6912]{1,0:T(8,128)}, f32[432]{0:T(512)}, /*inde...) custom-call(bf16[4,72,864]{2,1,0:T(8,128)(2,1)} %get-tuple-element.8, ...), custom_call_target="tpu_custom_call" | custom-call | tf_op jit(solution)/shard_map/assemble/pallas_call | solution.py:1786

commit v3 on v2

--- a/solution.py
+++ b/solution.py
@@ -1145,7 +1145,7 @@
     loads.wait(4, 5, 6, 7, 8)
 
     mix_sum.wait()
-    step_back = min(32, L)
+    step_back = min(128, L)
     mod_sums[...] = jnp.zeros_like(mod_sums)
     grad_b_out[...] = jnp.zeros_like(grad_b_out)
 
@@ -1605,7 +1605,7 @@
     one.relay()
     mix_sum.wait()
     loads.wait(7, 8, 9)
-    step = min(32, L)
+    step = min(128, L)
     mod_sums[...] = sums_in[...]
     scale = mod[1:2, :]
 

time: 266 us -> 264 us (level)
  no operation moved by 1% of the time
where the time goes in v3:
time: 264 us
  Pallas kernels  263 us (100%)
    pallas_call x1, Pallas kernels, forward(): pl.pallas_call(lambda *refs: forward_kernel(sizes, *refs), name='forward'...  116 us
    pallas_call x1, Pallas kernels, backward(): pl.pallas_call(lambda *refs: backward_kernel(sizes, *refs), name='backwar...  99.4 us
    pallas_call x1, Pallas kernels, mlp(): pl.pallas_call(lambda *refs: mlp_kernel(sizes, *refs), name='mlp', out_sh...  42 us
    pallas_call x1, Pallas kernels, assemble(): pl.pallas_call(lambda *refs: assemble_kernel(sizes, *refs), name='assembl...  5.56 us

profile of v3, /device:TPU:0, one launch (start us, length us, event | category | flops | bytes accessed | tf_op | source)
XLA Modules:
  0.0 264.0 jit_solution(17963489065614418912)
XLA Ops:
  0.6 116.1 %forward.1 = (bf16[4,256,1152]{2,1,0:T(8,128)(2,1)}, bf16[12,1024,128]{2,1,0:T(8,128)(2,1)}, bf16[256,1152]{1,0:T(8,128)(2,1)}, f32[256,1152]{1,0:T(8,128)}, bf1...) custom-call(bf16[1,1152]{1,0:T(2,128)(2,1)} %refs_6_.1, ...), custom_call_target="tpu_custom_call" | custom-call | tf_op jit(solution)/shard_map/forward/pallas_call | solution.py:762
  116.8 42.0 %mlp.1 = (bf16[256,1152]{1,0:T(8,128)(2,1)}, f32[256,1152]{1,0:T(8,128)}, bf16[4,256,288]{2,1,0:T(8,128)(2,1)}, bf16[1152,1152]{1,0:T(8,128)(2,1)}, bf16[4,72,11...) custom-call(f32[6,1152]{1,0:T(8,128)} %get-tuple-element.62.refs_0_., ...), custom_call_target="tpu_custom_call" | custom-call | tf_op jit(solution)/shard_map/mlp/pallas_call | solution.py:1217
  158.9 99.4 %backward.1 = (f32[256,1152]{1,0:T(8,128)}, bf16[4,72,864]{2,1,0:T(8,128)(2,1)}, bf16[4,72,1152]{2,1,0:T(8,128)(2,1)}, bf16[2,72,1152]{2,1,0:T(8,128)(2,1)}, bf1...) custom-call(f32[4,4,1,256]{3,2,1,0:T(1,128)} %get-tuple-element.61.r, ...), custom_call_target="tpu_custom_call" | custom-call | tf_op jit(solution)/shard_map/backward/pallas_call | solution.py:1673
  258.2 5.6 %assemble.1 = (bf16[256,1152]{1,0:T(8,128)(2,1)}, f32[256,1152]{1,0:T(8,128)}, f32[1,1152]{1,0:T(1,128)}, f32[72,6912]{1,0:T(8,128)}, f32[432]{0:T(512)}, /*inde...) custom-call(bf16[4,72,864]{2,1,0:T(8,128)(2,1)} %get-tuple-element.8, ...), custom_call_target="tpu_custom_call" | custom-call | tf_op jit(solution)/shard_map/assemble/pallas_call | solution.py:1786
